TPU v7x, 32 devices: a whole 2x2x4 slice. The times are simulated.
32 devices in a mesh: wide: 8 (over y, x, core), narrow: 4 (over z).
Axes of the slice: x: 2, y: 2, z: 4, core: 2. Of those that a mesh axis runs over, the one named last changes fastest.
Arguments:
- vectors: bfloat16 [3, 4096, 128], P(None, ('wide', 'narrow')), may hold values from -18 to 18
- hessian: bfloat16 [3, 3, 61, 4096], P(None, None, None, ('wide', 'narrow')), may hold values from -0.9 to 5.4
- neighbours: int32 [60, 4096], P(None, ('wide', 'narrow')), may hold values from 0 to 415
- halo_atoms: int32 [1024], P(('wide', 'narrow')), may hold values from 0 to 127
- labels: int32 [4096], P(('wide', 'narrow')), may hold values from 0 to 15
- masses: float32 [2, 16], replicated, may hold values from 1 to 32
- rotation: float32 [2, 128, 128], replicated, may hold values from -0.5 to 0.5
Outputs:
- gram: float32 [2, 128, 128], replicated
- rotated: bfloat16 [2, 3, 4096, 128], P(None, None, ('wide', 'narrow'))
Inputs may be any that keep to these rules, and one draw needn't show every extreme that they name: `neighbours`: A row below 128 is a local atom of the domain; a row r at or above it is boundary atom (r - 128) % 32 of block (r - 128) // 32 in the 3x3 order of the steps.
All inputs are finite; a program needn't handle non-finite values.
Results may differ from a plain program's by a relative error of at most 0.003.
Values may be sent and summed in bfloat16 or wider, within the bound.
No kernel may reach another device: no remote copies, remote signals or barrier semaphores. Data moves between devices by JAX's collectives and lax.ppermute only.
A program may use at most 64 MiB of HBM per device.

v0:
```python
import jax
import jax.numpy as jnp
from jax import lax
from jax.sharding import PartitionSpec as P


def padded(array, sides, width):
    for axis, dim in sides:
        size, length = (lax.axis_size(axis), array.shape[dim])
        up = [(i, (i + 1) % size) for i in range(size - 1)]
        down = [(j, i) for i, j in up]
        last = lax.slice_in_dim(array, length - width, length, axis=dim)
        leading = lax.slice_in_dim(array, 0, width, axis=dim)
        before = lax.ppermute(last, axis, up)
        after = lax.ppermute(leading, axis, down)
        array = jnp.concatenate([before, array, after], axis=dim)
    return array


def class_factors(inverse_roots, classes):
    onehot = (
        classes[None, :] == jnp.arange(inverse_roots.shape[1], dtype=jnp.int32)[:, None]
    ).astype(jnp.float32)
    return jnp.dot(inverse_roots, onehot, precision=lax.Precision.HIGHEST)


def scale_rows(rows_full, factors):
    return jnp.concatenate(
        [rows_full * factors[0][None, :, None], rows_full * factors[1][None, :, None]], axis=2
    ).astype(jnp.bfloat16)


def local(vectors, hessian, neighbours, halo_atoms, labels, masses, rotation):
    atoms_here = vectors.shape[1]
    width = vectors.shape[2]
    boundary = halo_atoms.shape[0]
    inverse_roots = lax.rsqrt(masses)
    factors = class_factors(inverse_roots, labels)
    vector_complete = vectors.astype(jnp.float32)
    scaled = scale_rows(vector_complete, factors)
    outgoing = jnp.take(scaled, halo_atoms, axis=1)[:, None, None]
    rims = padded(outgoing, (("wide", 1), ("narrow", 2)), 1)
    rim_rows = rims.reshape(3, 9 * boundary, 2 * width)
    extended = jnp.concatenate([scaled, rim_rows], axis=1)
    total = jnp.einsum("ija,jac->iac", hessian[:, :, 0], scaled, preferred_element_type=jnp.float32)

    def add_group(group, running):
        blocks = lax.dynamic_slice_in_dim(hessian, 1 + group * 4, 4, 2)
        indices = lax.dynamic_slice_in_dim(neighbours, group * 4, 4, 0)
        picked = jnp.take(extended, indices.reshape(-1), axis=1).reshape(
            3, 4, atoms_here, 2 * width
        )
        return running + jnp.einsum(
            "ijka,jkac->iac", blocks, picked, preferred_element_type=jnp.float32
        )

    total = lax.fori_loop(0, neighbours.shape[0] // 4, add_group, total)
    hydrogen_image = total[:, :, :width] * factors[0][None, :, None]
    deuterium_image = total[:, :, width:] * factors[1][None, :, None]
    partial_gram = jnp.stack(
        [
            jnp.einsum(
                "eqv,eqh->vh", vector_complete, hydrogen_image, precision=lax.Precision.HIGHEST
            ),
            jnp.einsum(
                "eqv,eqh->vh", vector_complete, deuterium_image, precision=lax.Precision.HIGHEST
            ),
        ]
    )
    atoms_all = 3.0 * atoms_here * lax.axis_size("wide") * lax.axis_size("narrow")
    images = (hydrogen_image, deuterium_image)
    gram = lax.psum(partial_gram, ("wide", "narrow")) / atoms_all
    outputs = []
    for isotope_variant in range(2):
        fresh_block = images[isotope_variant] - jnp.einsum(
            "jyx,xs->jys", vector_complete, gram[isotope_variant], precision=lax.Precision.HIGHEST
        )
        outputs.append(
            jnp.einsum(
                "jyx,xs->jys",
                fresh_block,
                rotation[isotope_variant],
                precision=lax.Precision.HIGHEST,
            ).astype(jnp.bfloat16)
        )
    return (gram, jnp.stack(outputs))


def solution(mesh):
    return jax.shard_map(
        local,
        mesh=mesh,
        in_specs=(
            P(None, ("wide", "narrow"), None),
            P(None, None, None, ("wide", "narrow")),
            P(None, ("wide", "narrow")),
            P(("wide", "narrow")),
            P(("wide", "narrow")),
            P(),
            P(),
        ),
        out_specs=(P(), P(None, None, ("wide", "narrow"), None)),
        check_vma=False,
    )
```

profile of v0, /device:TPU:0, one launch (start us, length us, event | category | flops | bytes accessed | tf_op | source)
XLA Modules:
  0.0 256.7 jit_solution(16522191547537341307)
XLA Ops:
  8.5 0.8 convolution_bitcast_fusion.6
  9.4 1.0 fusion.8
  11.3 1.3 collective-permute-start.1
  12.6 3.0 %collective-permute-start = (bf16[3,1,1,32,256]{4,0,3,2,1:T(4,128)(2,1)S(1)}, bf16[3,1,1,32,256]{4,0,3,2,1:T(4,128)(2,1)S(1)}, u32[]{:S(2)}, u32[]{:S(2)}) collective-permute-start(bf16[3,1,1,32,256]{4,0,3,2,1:T(4,128)(2,1)S(1)} %bitcast_select_fusion), channel_id=1, source_target_pairs={{0,4},{4,8},{8,12},{12,16},{16,20},{20,24},{24,28},{1,5},{5,9},{9,... | collective-permute-start | bytes 147464 | tf_op jit(solution)/shard_map/ppermute | solution.py:14
  15.7 0.7 slice.31
  16.8 1.3 collective-permute-start.3
  18.1 5.6 %collective-permute-start.2 = (bf16[3,3,1,32,256]{4,0,3,2,1:T(4,128)(2,1)S(1)}, bf16[3,3,1,32,256]{4,0,3,2,1:T(4,128)(2,1)S(1)}, u32[]{:S(2)}, u32[]{:S(2)}) collective-permute-start(bf16[3,3,1,32,256]{4,0,3,2,1:T(4,128)(2,1)S(1)} %pad_maximum_fusion.3), channel_id=1, source_target_pairs={{0,1},{1,2},{2,3},{4,5},{5,6},{6,7},{8,9},{9,10},{10,11},{12,13},{... | collective-permute-start | bytes 442376 | tf_op jit(solution)/shard_map/ppermute | solution.py:14
  24.0 2.6 %collective-permute-done.3 = bf16[3,3,1,32,256]{4,0,3,2,1:T(4,128)(2,1)S(1)} collective-permute-done((bf16[3,3,1,32,256]{4,0,3,2,1:T(4,128)(2,1)S(1)}, bf16[3,3,1,32,256]{4,0,3,2,1:T(4,128)(2,1)S(1)}, u32[]{:S(2)}, u32[]{:S(2)}) %collective-permute-start.3) | collective-permute-done | bytes 147488 | tf_op jit(solution)/shard_map/ppermute | solution.py:15
  26.5 1.7 collective-permute-done.2
  29.5 86.3 %while.15 = (s32[]{:T(128)}, f32[3,128,256]{2,0,1:T(4,128)S(1)}, s32[60,128]{1,0:T(8,128)}, bf16[3,416,256]{2,0,1:T(4,128)(2,1)S(1)}, bf16[3,3,61,128]{3,2,1,0:T...) while((s32[]{:T(128)}, f32[3,128,256]{2,0,1:T(4,128)S(1)}, ...), condition=%wide.region_1.2_spmd, body=%wide.region_0.1_spmd.sunk | while | flops 2856458 | bytes 3210441 | solution.py:57
  29.5 0.7 compare_and_fusion.3
  30.3 0.8 constant_dynamic-slice_fusion.4
  31.5 2.4 gather_fusion
  33.9 1.4 fusion.30
  35.3 0.7 compare_and_fusion.3
  36.0 0.8 constant_dynamic-slice_fusion.4
  37.2 2.4 gather_fusion
  39.6 1.4 fusion.30
  41.1 0.7 compare_and_fusion.3
  41.8 0.8 constant_dynamic-slice_fusion.4
  43.0 2.4 gather_fusion
  45.4 1.4 fusion.30
  46.8 0.7 compare_and_fusion.3
  47.5 0.8 constant_dynamic-slice_fusion.4
  48.7 2.4 gather_fusion
  51.1 1.4 fusion.30
  52.6 0.7 compare_and_fusion.3
  53.3 0.8 constant_dynamic-slice_fusion.4
  54.5 2.4 gather_fusion
  56.9 1.4 fusion.30
  58.3 0.7 compare_and_fusion.3
  59.0 0.8 constant_dynamic-slice_fusion.4
  60.2 2.4 gather_fusion
  62.7 1.4 fusion.30
  64.8 0.8 constant_dynamic-slice_fusion.4
  66.0 2.4 gather_fusion
  68.4 1.4 fusion.30
  70.6 0.8 constant_dynamic-slice_fusion.4
  71.8 2.4 gather_fusion
  74.2 1.4 fusion.30
  76.3 0.8 constant_dynamic-slice_fusion.4
  77.5 2.4 gather_fusion
  79.9 1.4 fusion.30
  82.1 0.8 constant_dynamic-slice_fusion.4
  83.3 2.4 gather_fusion
  85.7 1.4 fusion.30
  87.8 0.8 constant_dynamic-slice_fusion.4
  89.0 2.4 gather_fusion
  91.4 1.4 fusion.30
  93.6 0.8 constant_dynamic-slice_fusion.4
  94.8 2.4 gather_fusion
  97.2 1.4 fusion.30
  99.3 0.8 constant_dynamic-slice_fusion.4
  100.5 2.4 gather_fusion
  102.9 1.4 fusion.30
  105.1 0.8 constant_dynamic-slice_fusion.4
  106.3 2.4 gather_fusion
  108.7 1.4 fusion.30
  110.8 0.7 constant_dynamic-slice_fusion.4
  112.0 2.4 gather_fusion
  114.4 1.4 fusion.30
  117.4 128.9 %all-reduce.2.cloned.1.call-done = f32[2,128,128]{1,2,0:T(8,128)} async-done(((f32[2,128,128]{1,2,0:T(8,128)}), f32[2,128,128]{1,2,0:T(8,128)}) %all-reduce.2.cloned.1.call-update) | async-done | bytes 131088 | tf_op jit(solution)/shard_map/psum | solution.py:72
  246.3 0.9 broadcast_multiply_fusion
  247.2 0.8 copy.58
  (101 shorter events, 20.0 us)
Async XLA Ops:
  7.2 239.1 %all-reduce.2.cloned.1.call-start = ((), (), s32[]{:S(2)}) async-start(), calls=%async_computation | async-start | bytes 262144 | tf_op jit(solution)/shard_map/psum | solution.py:72
  11.3 5.3 %collective-permute-start.1 = (bf16[3,1,1,32,256]{4,0,3,2,1:T(4,128)(2,1)S(1)}, bf16[3,1,1,32,256]{4,0,3,2,1:T(4,128)(2,1)S(1)}, u32[]{:S(2)}, u32[]{:S(2)}) collective-permute-start(bf16[3,1,1,32,256]{4,0,3,2,1:T(4,128)(2,1)S(1)} %bitcast_select_fusion), channel_id=1, source_target_pairs={{4,0},{8,4},{12,8},{16,12},{20,16},{24,20},{28,24},{5,1},{9,5},{13... | collective-permute-start | bytes 147464 | tf_op jit(solution)/shard_map/ppermute | solution.py:15
  12.6 4.0 %collective-permute-start = (bf16[3,1,1,32,256]{4,0,3,2,1:T(4,128)(2,1)S(1)}, bf16[3,1,1,32,256]{4,0,3,2,1:T(4,128)(2,1)S(1)}, u32[]{:S(2)}, u32[]{:S(2)}) collective-permute-start(bf16[3,1,1,32,256]{4,0,3,2,1:T(4,128)(2,1)S(1)} %bitcast_select_fusion), channel_id=1, source_target_pairs={{0,4},{4,8},{8,12},{12,16},{16,20},{20,24},{24,28},{1,5},{5,9},{9,... | collective-permute-start | bytes 147464 | tf_op jit(solution)/shard_map/ppermute | solution.py:14
  16.8 9.8 %collective-permute-start.3 = (bf16[3,3,1,32,256]{4,0,3,2,1:T(4,128)(2,1)S(1)}, bf16[3,3,1,32,256]{4,0,3,2,1:T(4,128)(2,1)S(1)}, u32[]{:S(2)}, u32[]{:S(2)}) collective-permute-start(bf16[3,3,1,32,256]{4,0,3,2,1:T(4,128)(2,1)S(1)} %pad_maximum_fusion.3), channel_id=1, source_target_pairs={{1,0},{2,1},{3,2},{5,4},{6,5},{7,6},{9,8},{10,9},{11,10},{13,12},{... | collective-permute-start | bytes 442376 | tf_op jit(solution)/shard_map/ppermute | solution.py:15
  18.1 10.2 %collective-permute-start.2 = (bf16[3,3,1,32,256]{4,0,3,2,1:T(4,128)(2,1)S(1)}, bf16[3,3,1,32,256]{4,0,3,2,1:T(4,128)(2,1)S(1)}, u32[]{:S(2)}, u32[]{:S(2)}) collective-permute-start(bf16[3,3,1,32,256]{4,0,3,2,1:T(4,128)(2,1)S(1)} %pad_maximum_fusion.3), channel_id=1, source_target_pairs={{0,1},{1,2},{2,3},{4,5},{5,6},{6,7},{8,9},{9,10},{10,11},{12,13},{... | collective-permute-start | bytes 442376 | tf_op jit(solution)/shard_map/ppermute | solution.py:14
  29.5 86.4 %copy-start = (bf16[3,128,128]{2,1,0:T(8,128)(2,1)S(1)}, bf16[3,128,128]{2,1,0:T(8,128)(2,1)}, u32[]{:S(2)}) copy-start(bf16[3,128,128]{2,1,0:T(8,128)(2,1)} %param.9) | copy-start | bytes 294916
  116.7 131.8 %copy-start.1 = (f32[2,128,128]{2,1,0:T(8,128)S(1)}, f32[2,128,128]{2,1,0:T(8,128)}, u32[]{:S(2)}) copy-start(f32[2,128,128]{2,1,0:T(8,128)} %param.15) | copy-start | bytes 393220
Sparse Core Ops, SparseCore 0:
  117.5 128.6 all-reduce.1
where the time goes:
time: 258 us; the launch traced here: 257 us
  waiting for transfers between devices  133 us (52%)
  local copies, waits for them, and re-layouts  56.9 us (22%)
  matrix products  24.1 us (9%)
  other arithmetic  16.2 us (6%)
  between operations  14.2 us (6%)
  starting transfers between devices  11.3 us (4%)
    psum x1, waiting for transfers between devices, local(): gram = lax.psum(partial_gram, ('wide', 'narrow')) / atoms_all  129 us
    gather x15, local copies, waits for them, and re-layouts, add_group(): jnp.take(extended, indices.reshape(-1), axis=1)  36 us
    dot_general x15, matrix products, add_group(): jnp.einsum('ijka,jkac->iac', blocks, picked, preferred_element_type=jnp.f...  21.1 us
    dynamic_slice x30, local copies, waits for them, and re-layouts, add_group(): blocks = lax.dynamic_slice_in_dim(hessian, 1 + group * 4, 4, 2)  15.7 us
    and x15, other arithmetic, add_group(): jnp.take(extended, indices.reshape(-1), axis=1)  10.6 us
    ppermute x2, starting transfers between devices, padded(): before = lax.ppermute(last, axis, up)  8.63 us
  transfers between devices with their start and end apart: 5, of which 3 were waited for; matrix products, arithmetic and copies ran while one was open for 0% of the time, Pallas kernels for 0%

commit v1 on v0

--- a/solution.py
+++ b/solution.py
@@ -69,7 +69,7 @@
     )
     atoms_all = 3.0 * atoms_here * lax.axis_size("wide") * lax.axis_size("narrow")
     images = (hydrogen_image, deuterium_image)
-    gram = lax.psum(partial_gram, ("wide", "narrow")) / atoms_all
+    gram = jnp.sum(lax.all_gather(partial_gram, ("wide", "narrow")), axis=0) / atoms_all
     outputs = []
     for isotope_variant in range(2):
         fresh_block = images[isotope_variant] - jnp.einsum(

time: 258 us -> 196 us (0.76)
  waiting for transfers between devices: 133 us -> 70.3 us
    psum x1 -> x0, waiting for transfers between devices: 129 us -> none  [local(): gram = lax.psum(partial_gram, ('wide', 'narrow')) / atoms_all]
    all_gather x0 -> x1, waiting for transfers between devices: none -> 66 us  [local(): lax.all_gather(partial_gram, ('wide', 'narrow'))]
  transfers between devices with their start and end apart: 5 -> 5, of which waited for: 3 -> 3; matrix products, arithmetic and copies ran while one was open for 0% -> 1% of each run, Pallas kernels for 0% -> 0%
where the time goes in v1:
time: 196 us; the launch traced here: 195 us
  waiting for transfers between devices  70.3 us (36%)
  local copies, waits for them, and re-layouts  57.8 us (29%)
  matrix products  23.2 us (12%)
  other arithmetic  17 us (9%)
  between operations  14.3 us (7%)
  starting transfers between devices  11.3 us (6%)
    all_gather x1, waiting for transfers between devices, local(): lax.all_gather(partial_gram, ('wide', 'narrow'))  66 us
    gather x15, local copies, waits for them, and re-layouts, add_group(): jnp.take(extended, indices.reshape(-1), axis=1)  36 us
    dot_general x15, matrix products, add_group(): jnp.einsum('ijka,jkac->iac', blocks, picked, preferred_element_type=jnp.f...  20.2 us
    dynamic_slice x30, local copies, waits for them, and re-layouts, add_group(): blocks = lax.dynamic_slice_in_dim(hessian, 1 + group * 4, 4, 2)  15.7 us
    and x15, other arithmetic, add_group(): jnp.take(extended, indices.reshape(-1), axis=1)  10.6 us
    ppermute x2, starting transfers between devices, padded(): before = lax.ppermute(last, axis, up)  8.63 us
  transfers between devices with their start and end apart: 5, of which 3 were waited for; matrix products, arithmetic and copies ran while one was open for 1% of the time, Pallas kernels for 0%

profile of v1, /device:TPU:0, one launch (start us, length us, event | category | flops | bytes accessed | tf_op | source)
XLA Modules:
  0.0 194.7 jit_solution(9379338001247940526)
XLA Ops:
  8.5 0.8 convolution_bitcast_fusion.6
  9.4 1.0 fusion.8
  11.3 1.3 collective-permute-start.1
  12.6 3.0 %collective-permute-start = (bf16[3,1,1,32,256]{4,0,3,2,1:T(4,128)(2,1)S(1)}, bf16[3,1,1,32,256]{4,0,3,2,1:T(4,128)(2,1)S(1)}, u32[]{:S(2)}, u32[]{:S(2)}) collective-permute-start(bf16[3,1,1,32,256]{4,0,3,2,1:T(4,128)(2,1)S(1)} %bitcast_select_fusion), channel_id=1, source_target_pairs={{0,4},{4,8},{8,12},{12,16},{16,20},{20,24},{24,28},{1,5},{5,9},{9,... | collective-permute-start | bytes 147464 | tf_op jit(solution)/shard_map/ppermute | solution.py:14
  15.7 0.7 slice.31
  16.8 1.3 collective-permute-start.3
  18.1 5.6 %collective-permute-start.2 = (bf16[3,3,1,32,256]{4,0,3,2,1:T(4,128)(2,1)S(1)}, bf16[3,3,1,32,256]{4,0,3,2,1:T(4,128)(2,1)S(1)}, u32[]{:S(2)}, u32[]{:S(2)}) collective-permute-start(bf16[3,3,1,32,256]{4,0,3,2,1:T(4,128)(2,1)S(1)} %pad_maximum_fusion.3), channel_id=1, source_target_pairs={{0,1},{1,2},{2,3},{4,5},{5,6},{6,7},{8,9},{9,10},{10,11},{12,13},{... | collective-permute-start | bytes 442376 | tf_op jit(solution)/shard_map/ppermute | solution.py:14
  24.0 2.6 %collective-permute-done.3 = bf16[3,3,1,32,256]{4,0,3,2,1:T(4,128)(2,1)S(1)} collective-permute-done((bf16[3,3,1,32,256]{4,0,3,2,1:T(4,128)(2,1)S(1)}, bf16[3,3,1,32,256]{4,0,3,2,1:T(4,128)(2,1)S(1)}, u32[]{:S(2)}, u32[]{:S(2)}) %collective-permute-start.3) | collective-permute-done | bytes 147488 | tf_op jit(solution)/shard_map/ppermute | solution.py:15
  26.5 1.7 collective-permute-done.2
  29.5 85.4 %while.15 = (s32[]{:T(128)}, f32[3,128,256]{2,0,1:T(4,128)S(1)}, s32[60,128]{1,0:T(8,128)}, bf16[3,416,256]{2,0,1:T(4,128)(2,1)S(1)}, bf16[3,3,61,128]{3,2,1,0:T...) while((s32[]{:T(128)}, f32[3,128,256]{2,0,1:T(4,128)S(1)}, ...), condition=%wide.region_1.2_spmd, body=%wide.region_0.1_spmd.sunk | while | flops 2856458 | bytes 3210441 | solution.py:57
  29.5 0.7 compare_and_fusion.3
  30.3 0.8 constant_dynamic-slice_fusion.4
  31.5 2.4 %gather_fusion = bf16[512,3,256]{2,1,0:T(4,128)(2,1)S(1)} fusion(bf16[3,416,256]{2,0,1:T(4,128)(2,1)S(1)} %get-tuple-element.240, s32[1024]{0:T(1024)S(1)} %pad_clamp_fusion.3), kind=kCustom, calls=%fused_computation.clone.1 | custom fusion | bytes 1574912 | tf_op jit(solution)/shard_map/while/body/eval_jaxpr/jit(_take)/gather | solution.py:50
  33.9 1.3 fusion.30
  35.3 0.7 compare_and_fusion.3
  36.0 0.8 constant_dynamic-slice_fusion.4
  37.2 2.4 %gather_fusion = bf16[512,3,256]{2,1,0:T(4,128)(2,1)S(1)} fusion(bf16[3,416,256]{2,0,1:T(4,128)(2,1)S(1)} %get-tuple-element.240, s32[1024]{0:T(1024)S(1)} %pad_clamp_fusion.3), kind=kCustom, calls=%fused_computation.clone.1 | custom fusion | bytes 1574912 | tf_op jit(solution)/shard_map/while/body/eval_jaxpr/jit(_take)/gather | solution.py:50
  39.6 1.3 fusion.30
  41.0 0.7 compare_and_fusion.3
  41.7 0.8 constant_dynamic-slice_fusion.4
  42.9 2.4 %gather_fusion = bf16[512,3,256]{2,1,0:T(4,128)(2,1)S(1)} fusion(bf16[3,416,256]{2,0,1:T(4,128)(2,1)S(1)} %get-tuple-element.240, s32[1024]{0:T(1024)S(1)} %pad_clamp_fusion.3), kind=kCustom, calls=%fused_computation.clone.1 | custom fusion | bytes 1574912 | tf_op jit(solution)/shard_map/while/body/eval_jaxpr/jit(_take)/gather | solution.py:50
  45.3 1.3 fusion.30
  46.6 0.7 compare_and_fusion.3
  47.4 0.8 constant_dynamic-slice_fusion.4
  48.6 2.4 %gather_fusion = bf16[512,3,256]{2,1,0:T(4,128)(2,1)S(1)} fusion(bf16[3,416,256]{2,0,1:T(4,128)(2,1)S(1)} %get-tuple-element.240, s32[1024]{0:T(1024)S(1)} %pad_clamp_fusion.3), kind=kCustom, calls=%fused_computation.clone.1 | custom fusion | bytes 1574912 | tf_op jit(solution)/shard_map/while/body/eval_jaxpr/jit(_take)/gather | solution.py:50
  51.0 1.3 fusion.30
  52.3 0.7 compare_and_fusion.3
  53.1 0.8 constant_dynamic-slice_fusion.4
  54.3 2.4 %gather_fusion = bf16[512,3,256]{2,1,0:T(4,128)(2,1)S(1)} fusion(bf16[3,416,256]{2,0,1:T(4,128)(2,1)S(1)} %get-tuple-element.240, s32[1024]{0:T(1024)S(1)} %pad_clamp_fusion.3), kind=kCustom, calls=%fused_computation.clone.1 | custom fusion | bytes 1574912 | tf_op jit(solution)/shard_map/while/body/eval_jaxpr/jit(_take)/gather | solution.py:50
  56.7 1.3 fusion.30
  58.8 0.8 constant_dynamic-slice_fusion.4
  60.0 2.4 %gather_fusion = bf16[512,3,256]{2,1,0:T(4,128)(2,1)S(1)} fusion(bf16[3,416,256]{2,0,1:T(4,128)(2,1)S(1)} %get-tuple-element.240, s32[1024]{0:T(1024)S(1)} %pad_clamp_fusion.3), kind=kCustom, calls=%fused_computation.clone.1 | custom fusion | bytes 1574912 | tf_op jit(solution)/shard_map/while/body/eval_jaxpr/jit(_take)/gather | solution.py:50
  62.4 1.3 fusion.30
  64.5 0.8 constant_dynamic-slice_fusion.4
  65.7 2.4 %gather_fusion = bf16[512,3,256]{2,1,0:T(4,128)(2,1)S(1)} fusion(bf16[3,416,256]{2,0,1:T(4,128)(2,1)S(1)} %get-tuple-element.240, s32[1024]{0:T(1024)S(1)} %pad_clamp_fusion.3), kind=kCustom, calls=%fused_computation.clone.1 | custom fusion | bytes 1574912 | tf_op jit(solution)/shard_map/while/body/eval_jaxpr/jit(_take)/gather | solution.py:50
  68.1 1.3 fusion.30
  70.2 0.8 constant_dynamic-slice_fusion.4
  71.4 2.4 %gather_fusion = bf16[512,3,256]{2,1,0:T(4,128)(2,1)S(1)} fusion(bf16[3,416,256]{2,0,1:T(4,128)(2,1)S(1)} %get-tuple-element.240, s32[1024]{0:T(1024)S(1)} %pad_clamp_fusion.3), kind=kCustom, calls=%fused_computation.clone.1 | custom fusion | bytes 1574912 | tf_op jit(solution)/shard_map/while/body/eval_jaxpr/jit(_take)/gather | solution.py:50
  73.8 1.3 fusion.30
  75.8 0.8 constant_dynamic-slice_fusion.4
  77.1 2.4 %gather_fusion = bf16[512,3,256]{2,1,0:T(4,128)(2,1)S(1)} fusion(bf16[3,416,256]{2,0,1:T(4,128)(2,1)S(1)} %get-tuple-element.240, s32[1024]{0:T(1024)S(1)} %pad_clamp_fusion.3), kind=kCustom, calls=%fused_computation.clone.1 | custom fusion | bytes 1574912 | tf_op jit(solution)/shard_map/while/body/eval_jaxpr/jit(_take)/gather | solution.py:50
  79.5 1.3 fusion.30
  81.5 0.8 constant_dynamic-slice_fusion.4
  82.7 2.4 %gather_fusion = bf16[512,3,256]{2,1,0:T(4,128)(2,1)S(1)} fusion(bf16[3,416,256]{2,0,1:T(4,128)(2,1)S(1)} %get-tuple-element.240, s32[1024]{0:T(1024)S(1)} %pad_clamp_fusion.3), kind=kCustom, calls=%fused_computation.clone.1 | custom fusion | bytes 1574912 | tf_op jit(solution)/shard_map/while/body/eval_jaxpr/jit(_take)/gather | solution.py:50
  85.2 1.3 fusion.30
  87.2 0.8 constant_dynamic-slice_fusion.4
  88.4 2.4 %gather_fusion = bf16[512,3,256]{2,1,0:T(4,128)(2,1)S(1)} fusion(bf16[3,416,256]{2,0,1:T(4,128)(2,1)S(1)} %get-tuple-element.240, s32[1024]{0:T(1024)S(1)} %pad_clamp_fusion.3), kind=kCustom, calls=%fused_computation.clone.1 | custom fusion | bytes 1574912 | tf_op jit(solution)/shard_map/while/body/eval_jaxpr/jit(_take)/gather | solution.py:50
  90.8 1.3 fusion.30
  92.9 0.8 constant_dynamic-slice_fusion.4
  94.1 2.4 %gather_fusion = bf16[512,3,256]{2,1,0:T(4,128)(2,1)S(1)} fusion(bf16[3,416,256]{2,0,1:T(4,128)(2,1)S(1)} %get-tuple-element.240, s32[1024]{0:T(1024)S(1)} %pad_clamp_fusion.3), kind=kCustom, calls=%fused_computation.clone.1 | custom fusion | bytes 1574912 | tf_op jit(solution)/shard_map/while/body/eval_jaxpr/jit(_take)/gather | solution.py:50
  96.5 1.3 fusion.30
  98.6 0.8 constant_dynamic-slice_fusion.4
  99.8 2.4 %gather_fusion = bf16[512,3,256]{2,1,0:T(4,128)(2,1)S(1)} fusion(bf16[3,416,256]{2,0,1:T(4,128)(2,1)S(1)} %get-tuple-element.240, s32[1024]{0:T(1024)S(1)} %pad_clamp_fusion.3), kind=kCustom, calls=%fused_computation.clone.1 | custom fusion | bytes 1574912 | tf_op jit(solution)/shard_map/while/body/eval_jaxpr/jit(_take)/gather | solution.py:50
  102.2 1.3 fusion.30
  104.3 0.8 constant_dynamic-slice_fusion.4
  105.5 2.4 %gather_fusion = bf16[512,3,256]{2,1,0:T(4,128)(2,1)S(1)} fusion(bf16[3,416,256]{2,0,1:T(4,128)(2,1)S(1)} %get-tuple-element.240, s32[1024]{0:T(1024)S(1)} %pad_clamp_fusion.3), kind=kCustom, calls=%fused_computation.clone.1 | custom fusion | bytes 1574912 | tf_op jit(solution)/shard_map/while/body/eval_jaxpr/jit(_take)/gather | solution.py:50
  107.9 1.3 fusion.30
  110.0 0.7 constant_dynamic-slice_fusion.4
  111.2 2.4 %gather_fusion = bf16[512,3,256]{2,1,0:T(4,128)(2,1)S(1)} fusion(bf16[3,416,256]{2,0,1:T(4,128)(2,1)S(1)} %get-tuple-element.240, s32[1024]{0:T(1024)S(1)} %pad_clamp_fusion.3), kind=kCustom, calls=%fused_computation.clone.1 | custom fusion | bytes 1574912 | tf_op jit(solution)/shard_map/while/body/eval_jaxpr/jit(_take)/gather | solution.py:50
  113.6 1.3 fusion.30
  115.9 0.8 copy.70
  116.7 66.0 %all-gather.3.cloned.1.call-done = f32[64,128,128]{2,1,0:T(8,128)} async-done(((f32[2,128,128]{2,1,0:T(8,128)}), f32[64,128,128]{2,1,0:T(8,128)}) %all-gather.3.cloned.1.call-update) | async-done | bytes 4194320 | tf_op jit(solution)/shard_map/all_gather | solution.py:72
  182.7 2.4 %reduce_sum.9 = f32[2,128,128]{2,1,0:T(8,128)S(1)} reduce(f32[32,2,128,128]{3,2,1,0:T(8,128)} %bitcast.87, f32[]{:T(128)} %constant.109.clone.1), dimensions={0}, to_apply=%region_2.3 | reduce | flops 1015808 | bytes 4325380 | tf_op jit(solution)/shard_map/reduce_sum | solution.py:72
  185.2 0.8 copy.74
  (104 shorter events, 20.2 us)
Async XLA Ops:
  7.2 175.5 %all-gather.3.cloned.1.call-start = ((), (), s32[]{:S(2)}) async-start(), calls=%async_computation | async-start | bytes 4325376 | tf_op jit(solution)/shard_map/all_gather | solution.py:72
  11.3 5.3 %collective-permute-start.1 = (bf16[3,1,1,32,256]{4,0,3,2,1:T(4,128)(2,1)S(1)}, bf16[3,1,1,32,256]{4,0,3,2,1:T(4,128)(2,1)S(1)}, u32[]{:S(2)}, u32[]{:S(2)}) collective-permute-start(bf16[3,1,1,32,256]{4,0,3,2,1:T(4,128)(2,1)S(1)} %bitcast_select_fusion), channel_id=1, source_target_pairs={{4,0},{8,4},{12,8},{16,12},{20,16},{24,20},{28,24},{5,1},{9,5},{13... | collective-permute-start | bytes 147464 | tf_op jit(solution)/shard_map/ppermute | solution.py:15
  12.6 4.0 %collective-permute-start = (bf16[3,1,1,32,256]{4,0,3,2,1:T(4,128)(2,1)S(1)}, bf16[3,1,1,32,256]{4,0,3,2,1:T(4,128)(2,1)S(1)}, u32[]{:S(2)}, u32[]{:S(2)}) collective-permute-start(bf16[3,1,1,32,256]{4,0,3,2,1:T(4,128)(2,1)S(1)} %bitcast_select_fusion), channel_id=1, source_target_pairs={{0,4},{4,8},{8,12},{12,16},{16,20},{20,24},{24,28},{1,5},{5,9},{9,... | collective-permute-start | bytes 147464 | tf_op jit(solution)/shard_map/ppermute | solution.py:14
  16.8 9.8 %collective-permute-start.3 = (bf16[3,3,1,32,256]{4,0,3,2,1:T(4,128)(2,1)S(1)}, bf16[3,3,1,32,256]{4,0,3,2,1:T(4,128)(2,1)S(1)}, u32[]{:S(2)}, u32[]{:S(2)}) collective-permute-start(bf16[3,3,1,32,256]{4,0,3,2,1:T(4,128)(2,1)S(1)} %pad_maximum_fusion.3), channel_id=1, source_target_pairs={{1,0},{2,1},{3,2},{5,4},{6,5},{7,6},{9,8},{10,9},{11,10},{13,12},{... | collective-permute-start | bytes 442376 | tf_op jit(solution)/shard_map/ppermute | solution.py:15
  18.1 10.2 %collective-permute-start.2 = (bf16[3,3,1,32,256]{4,0,3,2,1:T(4,128)(2,1)S(1)}, bf16[3,3,1,32,256]{4,0,3,2,1:T(4,128)(2,1)S(1)}, u32[]{:S(2)}, u32[]{:S(2)}) collective-permute-start(bf16[3,3,1,32,256]{4,0,3,2,1:T(4,128)(2,1)S(1)} %pad_maximum_fusion.3), channel_id=1, source_target_pairs={{0,1},{1,2},{2,3},{4,5},{5,6},{6,7},{8,9},{9,10},{10,11},{12,13},{... | collective-permute-start | bytes 442376 | tf_op jit(solution)/shard_map/ppermute | solution.py:14
  29.5 85.5 %copy-start = (bf16[3,128,128]{2,1,0:T(8,128)(2,1)S(1)}, bf16[3,128,128]{2,1,0:T(8,128)(2,1)}, u32[]{:S(2)}) copy-start(bf16[3,128,128]{2,1,0:T(8,128)(2,1)} %param.9) | copy-start | bytes 294916
  185.1 1.4 copy-start.1
Sparse Core Ops, SparseCore 0:
  116.8 65.8 all-gather.2
